TPU v7x, 512 devices: a whole 4x8x8 slice. The times are simulated.
512 devices in a mesh: tm: 32 (over y, x), space: 16 (over z, core).
Axes of the slice: x: 4, y: 8, z: 8, core: 2. Of those that a mesh axis runs over, the one named last changes fastest.
Arguments:
- initial: float32 [64, 64, 128], P('space'), may hold values from -6 to 6
- starts: float32 [32, 64, 64, 128], P('tm', 'space'), may hold values from -6 to 6
- conductivity: float32 [64, 64, 128], P('space'), may hold values from 3e-05 to 0.26
Outputs:
- corrected: float32 [32, 64, 64, 128], P('tm', 'space')
- relaxed: float32 [32, 64, 64, 128], P('tm', 'space')
All inputs are finite; a program needn't handle non-finite values.
Results may differ from a plain program's by a relative error of at most 0.000023.
Values sent between devices are 32-bit elements; how exact they have to be, the bound alone decides.
A program may use at most 64 MiB of HBM per device.

v0:
```python
import jax
import jax.numpy as jnp
from jax import lax
from jax.sharding import PartitionSpec as P

STEPS = 16


FACE_WEIGHTS = (1.0, 1.0, 0.25, 0.25, 0.25, 0.25)


def padded_2(value, sides, width):
    for axis, dim in sides:
        count, length = (lax.axis_size(axis), value.shape[dim])
        up = [(i, (i + 1) % count) for i in range(count - 1)]
        down = [(j, i) for i, j in up]
        last = lax.slice_in_dim(value, length - width, length, axis=dim)
        initial = lax.slice_in_dim(value, 0, width, axis=dim)
        before = lax.ppermute(last, axis, up)
        after = lax.ppermute(initial, axis, down)
        value = jnp.concatenate([before, value, after], axis=dim)
    return value


def from_behind(block, axis, distance):
    devices = range(lax.axis_size(axis))
    route = [(i - distance, i) for i in devices if i - distance in devices]
    return lax.ppermute(block, axis, route)


def entering(value, axis, combine, identity):
    count, position = (lax.axis_size(axis), lax.axis_index(axis))
    everything = jax.tree.map(lambda part: lax.all_gather(part, axis), value)
    start = jax.tree.map(
        lambda part, zero: jnp.broadcast_to(jnp.asarray(zero, part.dtype), part.shape),
        value,
        identity,
    )

    def hop(k, before):
        reached = k < position
        new = combine(before, jax.tree.map(lambda part: part[k], everything))
        return jax.tree.map(lambda a, b: jnp.where(reached, a, b), new, before)

    return lax.fori_loop(0, count, hop, start)


def neighbours(padded):
    return (
        padded[2:, 1:-1, 1:-1],
        padded[:-2, 1:-1, 1:-1],
        padded[1:-1, 2:, 1:-1],
        padded[1:-1, :-2, 1:-1],
        padded[1:-1, 1:-1, 2:],
        padded[1:-1, 1:-1, :-2],
    )


def advance(current, diffusivity):
    scaled = diffusivity * (1.0 + 0.25 * jnp.tanh(current))
    pad_widths = ((0, 0), (1, 1), (1, 1))
    padded = jnp.pad(current, pad_widths)
    padded_scaled = jnp.pad(scaled, pad_widths)
    centre = padded[1:-1, 1:-1, 1:-1]
    centre_scaled = padded_scaled[1:-1, 1:-1, 1:-1]
    change = jnp.zeros_like(centre)
    for beside, beside_scaled, factor in zip(
        neighbours(padded), neighbours(padded_scaled), FACE_WEIGHTS
    ):
        change = change + factor * 0.5 * (centre_scaled + beside_scaled) * (beside - centre)
    return centre + change


def compose(earlier, latter):
    return (earlier[0] * latter[0], latter[0] * earlier[1] + latter[1])


def on_device(initial, starts, conductivity):
    position = lax.axis_index("tm")
    cond_wide = padded_2(conductivity, (("space", 0),), 1)

    def relax_block(current):

        def single_step(counter, values):
            widened = padded_2(values, (("space", 0),), 1)
            return advance(widened, cond_wide)

        return lax.fori_loop(0, STEPS, single_step, current)

    block_ends = relax_block(starts[0])[None]
    shifted = from_behind(block_ends, "tm", 1)
    previous = jnp.where(position == 0, initial[None], shifted)
    jump_terms = (previous - starts)[0]
    damping = 1.0 / (1.0 + STEPS * 3.0 * conductivity)
    powers, before = entering(
        (damping, jump_terms), "tm", compose, (jnp.ones_like(damping), jnp.zeros_like(damping))
    )
    errors = damping * before + jump_terms
    corrected = starts + errors[None]
    relaxed = relax_block(corrected[0])[None]
    return (corrected, relaxed)


def solution(mesh):
    in_specs = (P("space", None, None), P("tm", "space", None, None), P("space", None, None))
    out_specs = (P("tm", "space", None, None), P("tm", "space", None, None))
    return jax.shard_map(
        on_device, mesh=mesh, in_specs=in_specs, out_specs=out_specs, check_vma=False
    )
```

profile of v0, /device:TPU:1, one launch (start us, length us, event | category | flops | bytes accessed | tf_op | source)
XLA Modules:
  0.0 441.8 jit_solution(1472829704645917009)
XLA Ops:
  8.0 5.4 %collective-permute-start.4 = (f32[1,64,128]{2,1,0:T(8,128)S(1)}, f32[1,64,128]{2,1,0:T(8,128)S(1)}, u32[]{:S(2)}, u32[]{:S(2)}) collective-permute-start(f32[1,64,128]{2,1,0:T(8,128)S(1)} %get-tuple-element.228), channel_id=1, source_target_pairs={{0,1},{1,2},{2,3},{3,4},{4,5},{5,6},{6,7},{7,8},{8,9},{9,10},{10,1... | collective-permute-start | bytes 98312 | tf_op jit(solution)/shard_map/ppermute | solution.py:19
  13.4 4.7 %collective-permute-start.5 = (f32[1,64,128]{2,1,0:T(8,128)S(1)}, f32[1,64,128]{2,1,0:T(8,128)S(1)}, u32[]{:S(2)}, u32[]{:S(2)}) collective-permute-start(f32[1,64,128]{2,1,0:T(8,128)S(1)} %get-tuple-element.227), channel_id=1, source_target_pairs={{1,0},{2,1},{3,2},{4,3},{5,4},{6,5},{7,6},{8,7},{9,8},{10,9},{11,1... | collective-permute-start | bytes 98312 | tf_op jit(solution)/shard_map/ppermute | solution.py:20
  20.7 139.7 %while.38 = (s32[]{:T(128)}, f32[4,64,128]{2,1,0:T(8,128)S(1)}, f32[6,64,128]{2,1,0:T(8,128)S(1)}, s32[]{:T(128)}) while((s32[]{:T(128)}, f32[4,64,128]{2,1,0:T(8,128)S(1)}, f32[6,64,128]{2,1,0:T(8,128)S(1)}, s32[]{:T(128)}) %tuple.86), condition=%wide.region_1.2_spmd, body=%wide.region_0.1_spmd.sunk | while | flops 1196034 | bytes 2752645 | solution.py:88
  22.8 2.4 collective-permute-start.1
  25.2 2.8 collective-permute-done.1
  30.2 2.4 collective-permute-start.1
  32.7 2.8 collective-permute-done.1
  37.7 2.4 collective-permute-start.1
  40.2 5.6 %collective-permute-done.1 = f32[1,64,128]{2,1,0:T(8,128)S(1)} collective-permute-done((f32[1,64,128]{2,1,0:T(8,128)S(1)}, f32[1,64,128]{2,1,0:T(8,128)S(1)}, u32[]{:S(2)}, u32[]{:S(2)}) %collective-permute-start.1) | collective-permute-done | bytes 32800 | tf_op jit(solution)/shard_map/while/body/eval_jaxpr/ppermute | solution.py:20
  48.0 2.4 collective-permute-start.1
  50.4 5.2 %collective-permute-done.1 = f32[1,64,128]{2,1,0:T(8,128)S(1)} collective-permute-done((f32[1,64,128]{2,1,0:T(8,128)S(1)}, f32[1,64,128]{2,1,0:T(8,128)S(1)}, u32[]{:S(2)}, u32[]{:S(2)}) %collective-permute-start.1) | collective-permute-done | bytes 32800 | tf_op jit(solution)/shard_map/while/body/eval_jaxpr/ppermute | solution.py:20
  57.8 2.4 collective-permute-start.1
  60.3 4.1 collective-permute-done.1
  66.6 2.4 collective-permute-start.1
  69.0 4.0 collective-permute-done.1
  75.3 2.4 collective-permute-start.1
  77.8 4.0 collective-permute-done.1
  84.0 2.4 collective-permute-start.1
  86.4 4.4 collective-permute-done.1
  93.1 2.4 collective-permute-start.1
  95.5 4.4 collective-permute-done.1
  102.1 2.4 collective-permute-start.1
  104.6 4.4 collective-permute-done.1
  111.2 2.4 collective-permute-start.1
  113.7 3.3 collective-permute-done.1
  119.2 2.4 collective-permute-start.1
  121.7 3.6 collective-permute-done.1
  127.6 2.4 collective-permute-start.1
  130.0 4.0 collective-permute-done.1
  136.2 2.4 collective-permute-start.1
  138.7 4.0 collective-permute-done.1
  144.9 2.4 collective-permute-start.1
  147.4 4.0 collective-permute-done.1
  153.6 2.4 collective-permute-start.1
  156.1 4.0 collective-permute-done.1
  160.3 3.5 collective-permute-start.6
  166.5 89.2 %all-gather.4.cloned.1.call-done = f32[32,4,64,128]{3,2,1,0:T(8,128)} async-done(((f32[1,4,64,128]{3,2,1,0:T(8,128)}), f32[32,4,64,128]{3,2,1,0:T(8,128)}) %all-gather.4.cloned.1.call-update) | async-done | bytes 4194320 | tf_op jit(solution)/shard_map/all_gather | solution.py:33
  255.7 34.9 %while.40 = (s32[]{:T(128)}, f32[4,64,128]{2,1,0:T(8,128)S(1)}, s32[]{:T(128)}, f32[32,4,64,128]{3,2,1,0:T(8,128)}, f32[32,4,64,128]{3,2,1,0:T(8,128)}, /*index=5*/s32[]{:T(128)}, s32[]{:T(128)}) while((s32[]{:T(128)}, f32[4,64,128]{2,1,0:T(8,128)S(1)}, s32[]{:T(128)}, f32[32,4,64,128]{3,2,1,0:T(8,128)}, ...), condition=%wide.region_3.4_spmd.clone, body=%wide.region_2.3_spmd.clone.sunk | while | flops 131076 | bytes 524389 | solution.py:45
  292.3 142.0 %while.39 = (s32[]{:T(128)}, f32[4,64,128]{2,1,0:T(8,128)S(1)}, f32[6,64,128]{2,1,0:T(8,128)S(1)}, s32[]{:T(128)}) while((s32[]{:T(128)}, f32[4,64,128]{2,1,0:T(8,128)S(1)}, f32[6,64,128]{2,1,0:T(8,128)S(1)}, s32[]{:T(128)}) %tuple.99), condition=%wide.region_5.6_spmd, body=%wide.region_4.5_spmd.sunk | while | flops 1196034 | bytes 2752645 | solution.py:88
  292.3 7.4 %collective-permute-start.2 = (f32[1,64,128]{2,1,0:T(8,128)S(1)}, f32[1,64,128]{2,1,0:T(8,128)S(1)}, u32[]{:S(2)}, u32[]{:S(2)}) collective-permute-start(f32[1,64,128]{2,1,0:T(8,128)S(1)} %get-tuple-element.299), channel_id=1, source_target_pairs={{0,1},{1,2},{2,3},{3,4},{4,5},{5,6},{6,7},{7,8},{8,9},{9,10},{10,1... | collective-permute-start | bytes 98312 | tf_op jit(solution)/shard_map/while/body/eval_jaxpr/ppermute | solution.py:19
  301.6 3.3 collective-permute-done.3
  307.1 2.4 collective-permute-start.3
  309.6 2.8 collective-permute-done.3
  314.6 2.4 collective-permute-start.3
  317.1 2.8 collective-permute-done.3
  322.1 2.4 collective-permute-start.3
  324.6 5.2 %collective-permute-done.3 = f32[1,64,128]{2,1,0:T(8,128)S(1)} collective-permute-done((f32[1,64,128]{2,1,0:T(8,128)S(1)}, f32[1,64,128]{2,1,0:T(8,128)S(1)}, u32[]{:S(2)}, u32[]{:S(2)}) %collective-permute-start.3) | collective-permute-done | bytes 32800 | tf_op jit(solution)/shard_map/while/body/eval_jaxpr/ppermute | solution.py:20
  332.0 2.4 collective-permute-start.3
  334.5 4.0 collective-permute-done.3
  340.7 2.4 collective-permute-start.3
  343.2 4.0 collective-permute-done.3
  349.4 2.4 collective-permute-start.3
  351.8 4.0 collective-permute-done.3
  360.5 4.0 collective-permute-done.3
  369.2 4.0 collective-permute-done.3
  375.4 2.4 collective-permute-start.3
  377.9 4.0 collective-permute-done.3
  386.6 4.0 collective-permute-done.3
  395.3 4.0 collective-permute-done.3
  404.0 4.0 collective-permute-done.3
  412.6 4.0 collective-permute-done.3
  421.3 4.0 collective-permute-done.3
  427.6 2.4 collective-permute-start.3
  430.0 4.0 collective-permute-done.3
  (354 shorter events, 130.2 us)
Async XLA Ops:
  7.2 159.3 %all-gather.6.cloned.1.call-start = ((), (), s32[]{:S(2)}) async-start(), calls=%async_computation.1 | async-start | bytes 4325376 | tf_op jit(solution)/shard_map/all_gather | solution.py:33
  8.0 11.0 %collective-permute-start.4 = (f32[1,64,128]{2,1,0:T(8,128)S(1)}, f32[1,64,128]{2,1,0:T(8,128)S(1)}, u32[]{:S(2)}, u32[]{:S(2)}) collective-permute-start(f32[1,64,128]{2,1,0:T(8,128)S(1)} %get-tuple-element.228), channel_id=1, source_target_pairs={{0,1},{1,2},{2,3},{3,4},{4,5},{5,6},{6,7},{7,8},{8,9},{9,10},{10,1... | collective-permute-start | bytes 98312 | tf_op jit(solution)/shard_map/ppermute | solution.py:19
  13.4 7.2 %collective-permute-start.5 = (f32[1,64,128]{2,1,0:T(8,128)S(1)}, f32[1,64,128]{2,1,0:T(8,128)S(1)}, u32[]{:S(2)}, u32[]{:S(2)}) collective-permute-start(f32[1,64,128]{2,1,0:T(8,128)S(1)} %get-tuple-element.227), channel_id=1, source_target_pairs={{1,0},{2,1},{3,2},{4,3},{5,4},{6,5},{7,6},{8,7},{9,8},{10,9},{11,1... | collective-permute-start | bytes 98312 | tf_op jit(solution)/shard_map/ppermute | solution.py:20
  20.6 235.1 %all-gather.4.cloned.1.call-start = ((), (), s32[]{:S(2)}) async-start(), calls=%async_computation | async-start | bytes 4325376 | tf_op jit(solution)/shard_map/all_gather | solution.py:33
  20.7 4.5 %collective-permute-start = (f32[1,64,128]{2,1,0:T(8,128)S(1)}, f32[1,64,128]{2,1,0:T(8,128)S(1)}, u32[]{:S(2)}, u32[]{:S(2)}) collective-permute-start(f32[1,64,128]{2,1,0:T(8,128)S(1)} %get-tuple-element.294), channel_id=1, source_target_pairs={{0,1},{1,2},{2,3},{3,4},{4,5},{5,6},{6,7},{7,8},{8,9},{9,10},{10,1... | collective-permute-start | bytes 98312 | tf_op jit(solution)/shard_map/while/body/eval_jaxpr/ppermute | solution.py:19
  22.8 5.2 %collective-permute-start.1 = (f32[1,64,128]{2,1,0:T(8,128)S(1)}, f32[1,64,128]{2,1,0:T(8,128)S(1)}, u32[]{:S(2)}, u32[]{:S(2)}) collective-permute-start(f32[1,64,128]{2,1,0:T(8,128)S(1)} %get-tuple-element.295), channel_id=1, source_target_pairs={{1,0},{2,1},{3,2},{4,3},{5,4},{6,5},{7,6},{8,7},{9,8},{10,9},{11,1... | collective-permute-start | bytes 98312 | tf_op jit(solution)/shard_map/while/body/eval_jaxpr/ppermute | solution.py:20
  28.3 4.3 collective-permute-start
  30.2 5.2 %collective-permute-start.1 = (f32[1,64,128]{2,1,0:T(8,128)S(1)}, f32[1,64,128]{2,1,0:T(8,128)S(1)}, u32[]{:S(2)}, u32[]{:S(2)}) collective-permute-start(f32[1,64,128]{2,1,0:T(8,128)S(1)} %get-tuple-element.295), channel_id=1, source_target_pairs={{1,0},{2,1},{3,2},{4,3},{5,4},{6,5},{7,6},{8,7},{9,8},{10,9},{11,1... | collective-permute-start | bytes 98312 | tf_op jit(solution)/shard_map/while/body/eval_jaxpr/ppermute | solution.py:20
  35.8 4.3 collective-permute-start
  37.7 8.0 %collective-permute-start.1 = (f32[1,64,128]{2,1,0:T(8,128)S(1)}, f32[1,64,128]{2,1,0:T(8,128)S(1)}, u32[]{:S(2)}, u32[]{:S(2)}) collective-permute-start(f32[1,64,128]{2,1,0:T(8,128)S(1)} %get-tuple-element.295), channel_id=1, source_target_pairs={{1,0},{2,1},{3,2},{4,3},{5,4},{6,5},{7,6},{8,7},{9,8},{10,9},{11,1... | collective-permute-start | bytes 98312 | tf_op jit(solution)/shard_map/while/body/eval_jaxpr/ppermute | solution.py:20
  46.0 4.3 collective-permute-start
  48.0 7.6 %collective-permute-start.1 = (f32[1,64,128]{2,1,0:T(8,128)S(1)}, f32[1,64,128]{2,1,0:T(8,128)S(1)}, u32[]{:S(2)}, u32[]{:S(2)}) collective-permute-start(f32[1,64,128]{2,1,0:T(8,128)S(1)} %get-tuple-element.295), channel_id=1, source_target_pairs={{1,0},{2,1},{3,2},{4,3},{5,4},{6,5},{7,6},{8,7},{9,8},{10,9},{11,1... | collective-permute-start | bytes 98312 | tf_op jit(solution)/shard_map/while/body/eval_jaxpr/ppermute | solution.py:20
  55.9 4.3 collective-permute-start
  57.8 6.5 %collective-permute-start.1 = (f32[1,64,128]{2,1,0:T(8,128)S(1)}, f32[1,64,128]{2,1,0:T(8,128)S(1)}, u32[]{:S(2)}, u32[]{:S(2)}) collective-permute-start(f32[1,64,128]{2,1,0:T(8,128)S(1)} %get-tuple-element.295), channel_id=1, source_target_pairs={{1,0},{2,1},{3,2},{4,3},{5,4},{6,5},{7,6},{8,7},{9,8},{10,9},{11,1... | collective-permute-start | bytes 98312 | tf_op jit(solution)/shard_map/while/body/eval_jaxpr/ppermute | solution.py:20
  64.7 4.3 collective-permute-start
  66.6 6.5 %collective-permute-start.1 = (f32[1,64,128]{2,1,0:T(8,128)S(1)}, f32[1,64,128]{2,1,0:T(8,128)S(1)}, u32[]{:S(2)}, u32[]{:S(2)}) collective-permute-start(f32[1,64,128]{2,1,0:T(8,128)S(1)} %get-tuple-element.295), channel_id=1, source_target_pairs={{1,0},{2,1},{3,2},{4,3},{5,4},{6,5},{7,6},{8,7},{9,8},{10,9},{11,1... | collective-permute-start | bytes 98312 | tf_op jit(solution)/shard_map/while/body/eval_jaxpr/ppermute | solution.py:20
  73.4 4.3 collective-permute-start
  75.3 6.4 %collective-permute-start.1 = (f32[1,64,128]{2,1,0:T(8,128)S(1)}, f32[1,64,128]{2,1,0:T(8,128)S(1)}, u32[]{:S(2)}, u32[]{:S(2)}) collective-permute-start(f32[1,64,128]{2,1,0:T(8,128)S(1)} %get-tuple-element.295), channel_id=1, source_target_pairs={{1,0},{2,1},{3,2},{4,3},{5,4},{6,5},{7,6},{8,7},{9,8},{10,9},{11,1... | collective-permute-start | bytes 98312 | tf_op jit(solution)/shard_map/while/body/eval_jaxpr/ppermute | solution.py:20
  82.0 4.3 collective-permute-start
  84.0 6.8 %collective-permute-start.1 = (f32[1,64,128]{2,1,0:T(8,128)S(1)}, f32[1,64,128]{2,1,0:T(8,128)S(1)}, u32[]{:S(2)}, u32[]{:S(2)}) collective-permute-start(f32[1,64,128]{2,1,0:T(8,128)S(1)} %get-tuple-element.295), channel_id=1, source_target_pairs={{1,0},{2,1},{3,2},{4,3},{5,4},{6,5},{7,6},{8,7},{9,8},{10,9},{11,1... | collective-permute-start | bytes 98312 | tf_op jit(solution)/shard_map/while/body/eval_jaxpr/ppermute | solution.py:20
  91.1 4.3 collective-permute-start
  93.1 6.8 %collective-permute-start.1 = (f32[1,64,128]{2,1,0:T(8,128)S(1)}, f32[1,64,128]{2,1,0:T(8,128)S(1)}, u32[]{:S(2)}, u32[]{:S(2)}) collective-permute-start(f32[1,64,128]{2,1,0:T(8,128)S(1)} %get-tuple-element.295), channel_id=1, source_target_pairs={{1,0},{2,1},{3,2},{4,3},{5,4},{6,5},{7,6},{8,7},{9,8},{10,9},{11,1... | collective-permute-start | bytes 98312 | tf_op jit(solution)/shard_map/while/body/eval_jaxpr/ppermute | solution.py:20
  100.2 4.3 collective-permute-start
  102.1 6.8 %collective-permute-start.1 = (f32[1,64,128]{2,1,0:T(8,128)S(1)}, f32[1,64,128]{2,1,0:T(8,128)S(1)}, u32[]{:S(2)}, u32[]{:S(2)}) collective-permute-start(f32[1,64,128]{2,1,0:T(8,128)S(1)} %get-tuple-element.295), channel_id=1, source_target_pairs={{1,0},{2,1},{3,2},{4,3},{5,4},{6,5},{7,6},{8,7},{9,8},{10,9},{11,1... | collective-permute-start | bytes 98312 | tf_op jit(solution)/shard_map/while/body/eval_jaxpr/ppermute | solution.py:20
  109.3 4.3 collective-permute-start
  111.2 5.8 %collective-permute-start.1 = (f32[1,64,128]{2,1,0:T(8,128)S(1)}, f32[1,64,128]{2,1,0:T(8,128)S(1)}, u32[]{:S(2)}, u32[]{:S(2)}) collective-permute-start(f32[1,64,128]{2,1,0:T(8,128)S(1)} %get-tuple-element.295), channel_id=1, source_target_pairs={{1,0},{2,1},{3,2},{4,3},{5,4},{6,5},{7,6},{8,7},{9,8},{10,9},{11,1... | collective-permute-start | bytes 98312 | tf_op jit(solution)/shard_map/while/body/eval_jaxpr/ppermute | solution.py:20
  117.3 4.3 collective-permute-start
  119.2 6.1 %collective-permute-start.1 = (f32[1,64,128]{2,1,0:T(8,128)S(1)}, f32[1,64,128]{2,1,0:T(8,128)S(1)}, u32[]{:S(2)}, u32[]{:S(2)}) collective-permute-start(f32[1,64,128]{2,1,0:T(8,128)S(1)} %get-tuple-element.295), channel_id=1, source_target_pairs={{1,0},{2,1},{3,2},{4,3},{5,4},{6,5},{7,6},{8,7},{9,8},{10,9},{11,1... | collective-permute-start | bytes 98312 | tf_op jit(solution)/shard_map/while/body/eval_jaxpr/ppermute | solution.py:20
  125.6 4.3 collective-permute-start
  127.6 6.4 %collective-permute-start.1 = (f32[1,64,128]{2,1,0:T(8,128)S(1)}, f32[1,64,128]{2,1,0:T(8,128)S(1)}, u32[]{:S(2)}, u32[]{:S(2)}) collective-permute-start(f32[1,64,128]{2,1,0:T(8,128)S(1)} %get-tuple-element.295), channel_id=1, source_target_pairs={{1,0},{2,1},{3,2},{4,3},{5,4},{6,5},{7,6},{8,7},{9,8},{10,9},{11,1... | collective-permute-start | bytes 98312 | tf_op jit(solution)/shard_map/while/body/eval_jaxpr/ppermute | solution.py:20
  134.3 4.3 collective-permute-start
  136.2 6.4 %collective-permute-start.1 = (f32[1,64,128]{2,1,0:T(8,128)S(1)}, f32[1,64,128]{2,1,0:T(8,128)S(1)}, u32[]{:S(2)}, u32[]{:S(2)}) collective-permute-start(f32[1,64,128]{2,1,0:T(8,128)S(1)} %get-tuple-element.295), channel_id=1, source_target_pairs={{1,0},{2,1},{3,2},{4,3},{5,4},{6,5},{7,6},{8,7},{9,8},{10,9},{11,1... | collective-permute-start | bytes 98312 | tf_op jit(solution)/shard_map/while/body/eval_jaxpr/ppermute | solution.py:20
  143.0 4.3 collective-permute-start
  144.9 6.4 %collective-permute-start.1 = (f32[1,64,128]{2,1,0:T(8,128)S(1)}, f32[1,64,128]{2,1,0:T(8,128)S(1)}, u32[]{:S(2)}, u32[]{:S(2)}) collective-permute-start(f32[1,64,128]{2,1,0:T(8,128)S(1)} %get-tuple-element.295), channel_id=1, source_target_pairs={{1,0},{2,1},{3,2},{4,3},{5,4},{6,5},{7,6},{8,7},{9,8},{10,9},{11,1... | collective-permute-start | bytes 98312 | tf_op jit(solution)/shard_map/while/body/eval_jaxpr/ppermute | solution.py:20
  151.7 4.3 collective-permute-start
  153.6 6.4 %collective-permute-start.1 = (f32[1,64,128]{2,1,0:T(8,128)S(1)}, f32[1,64,128]{2,1,0:T(8,128)S(1)}, u32[]{:S(2)}, u32[]{:S(2)}) collective-permute-start(f32[1,64,128]{2,1,0:T(8,128)S(1)} %get-tuple-element.295), channel_id=1, source_target_pairs={{1,0},{2,1},{3,2},{4,3},{5,4},{6,5},{7,6},{8,7},{9,8},{10,9},{11,1... | collective-permute-start | bytes 98312 | tf_op jit(solution)/shard_map/while/body/eval_jaxpr/ppermute | solution.py:20
  160.3 5.4 %collective-permute-start.6 = (f32[1,4,64,128]{3,2,1,0:T(8,128)S(1)}, f32[1,4,64,128]{3,2,1,0:T(8,128)S(1)}, u32[]{:S(2)}, u32[]{:S(2)}) collective-permute-start(f32[1,4,64,128]{3,2,1,0:T(8,128)S(1)} %bitcast.27), channel_id=1, source_target_pairs={{0,16},{16,32},{32,48},{48,64},{64,80},{80,96},{96,112},{112,128},... | collective-permute-start | bytes 393224 | tf_op jit(solution)/shard_map/ppermute | solution.py:28
  292.3 9.3 %collective-permute-start.2 = (f32[1,64,128]{2,1,0:T(8,128)S(1)}, f32[1,64,128]{2,1,0:T(8,128)S(1)}, u32[]{:S(2)}, u32[]{:S(2)}) collective-permute-start(f32[1,64,128]{2,1,0:T(8,128)S(1)} %get-tuple-element.299), channel_id=1, source_target_pairs={{0,1},{1,2},{2,3},{3,4},{4,5},{5,6},{6,7},{7,8},{8,9},{9,10},{10,1... | collective-permute-start | bytes 98312 | tf_op jit(solution)/shard_map/while/body/eval_jaxpr/ppermute | solution.py:19
  299.7 5.2 %collective-permute-start.3 = (f32[1,64,128]{2,1,0:T(8,128)S(1)}, f32[1,64,128]{2,1,0:T(8,128)S(1)}, u32[]{:S(2)}, u32[]{:S(2)}) collective-permute-start(f32[1,64,128]{2,1,0:T(8,128)S(1)} %get-tuple-element.300), channel_id=1, source_target_pairs={{1,0},{2,1},{3,2},{4,3},{5,4},{6,5},{7,6},{8,7},{9,8},{10,9},{11,1... | collective-permute-start | bytes 98312 | tf_op jit(solution)/shard_map/while/body/eval_jaxpr/ppermute | solution.py:20
  305.2 4.3 collective-permute-start.2
  307.1 5.2 %collective-permute-start.3 = (f32[1,64,128]{2,1,0:T(8,128)S(1)}, f32[1,64,128]{2,1,0:T(8,128)S(1)}, u32[]{:S(2)}, u32[]{:S(2)}) collective-permute-start(f32[1,64,128]{2,1,0:T(8,128)S(1)} %get-tuple-element.300), channel_id=1, source_target_pairs={{1,0},{2,1},{3,2},{4,3},{5,4},{6,5},{7,6},{8,7},{9,8},{10,9},{11,1... | collective-permute-start | bytes 98312 | tf_op jit(solution)/shard_map/while/body/eval_jaxpr/ppermute | solution.py:20
  312.7 4.3 collective-permute-start.2
  314.6 5.2 %collective-permute-start.3 = (f32[1,64,128]{2,1,0:T(8,128)S(1)}, f32[1,64,128]{2,1,0:T(8,128)S(1)}, u32[]{:S(2)}, u32[]{:S(2)}) collective-permute-start(f32[1,64,128]{2,1,0:T(8,128)S(1)} %get-tuple-element.300), channel_id=1, source_target_pairs={{1,0},{2,1},{3,2},{4,3},{5,4},{6,5},{7,6},{8,7},{9,8},{10,9},{11,1... | collective-permute-start | bytes 98312 | tf_op jit(solution)/shard_map/while/body/eval_jaxpr/ppermute | solution.py:20
  320.2 4.3 collective-permute-start.2
  322.1 7.7 %collective-permute-start.3 = (f32[1,64,128]{2,1,0:T(8,128)S(1)}, f32[1,64,128]{2,1,0:T(8,128)S(1)}, u32[]{:S(2)}, u32[]{:S(2)}) collective-permute-start(f32[1,64,128]{2,1,0:T(8,128)S(1)} %get-tuple-element.300), channel_id=1, source_target_pairs={{1,0},{2,1},{3,2},{4,3},{5,4},{6,5},{7,6},{8,7},{9,8},{10,9},{11,1... | collective-permute-start | bytes 98312 | tf_op jit(solution)/shard_map/while/body/eval_jaxpr/ppermute | solution.py:20
  330.1 4.3 collective-permute-start.2
  332.0 6.4 %collective-permute-start.3 = (f32[1,64,128]{2,1,0:T(8,128)S(1)}, f32[1,64,128]{2,1,0:T(8,128)S(1)}, u32[]{:S(2)}, u32[]{:S(2)}) collective-permute-start(f32[1,64,128]{2,1,0:T(8,128)S(1)} %get-tuple-element.300), channel_id=1, source_target_pairs={{1,0},{2,1},{3,2},{4,3},{5,4},{6,5},{7,6},{8,7},{9,8},{10,9},{11,1... | collective-permute-start | bytes 98312 | tf_op jit(solution)/shard_map/while/body/eval_jaxpr/ppermute | solution.py:20
  340.7 6.4 %collective-permute-start.3 = (f32[1,64,128]{2,1,0:T(8,128)S(1)}, f32[1,64,128]{2,1,0:T(8,128)S(1)}, u32[]{:S(2)}, u32[]{:S(2)}) collective-permute-start(f32[1,64,128]{2,1,0:T(8,128)S(1)} %get-tuple-element.300), channel_id=1, source_target_pairs={{1,0},{2,1},{3,2},{4,3},{5,4},{6,5},{7,6},{8,7},{9,8},{10,9},{11,1... | collective-permute-start | bytes 98312 | tf_op jit(solution)/shard_map/while/body/eval_jaxpr/ppermute | solution.py:20
  349.4 6.4 %collective-permute-start.3 = (f32[1,64,128]{2,1,0:T(8,128)S(1)}, f32[1,64,128]{2,1,0:T(8,128)S(1)}, u32[]{:S(2)}, u32[]{:S(2)}) collective-permute-start(f32[1,64,128]{2,1,0:T(8,128)S(1)} %get-tuple-element.300), channel_id=1, source_target_pairs={{1,0},{2,1},{3,2},{4,3},{5,4},{6,5},{7,6},{8,7},{9,8},{10,9},{11,1... | collective-permute-start | bytes 98312 | tf_op jit(solution)/shard_map/while/body/eval_jaxpr/ppermute | solution.py:20
  356.1 4.3 collective-permute-start.2
  358.1 6.4 %collective-permute-start.3 = (f32[1,64,128]{2,1,0:T(8,128)S(1)}, f32[1,64,128]{2,1,0:T(8,128)S(1)}, u32[]{:S(2)}, u32[]{:S(2)}) collective-permute-start(f32[1,64,128]{2,1,0:T(8,128)S(1)} %get-tuple-element.300), channel_id=1, source_target_pairs={{1,0},{2,1},{3,2},{4,3},{5,4},{6,5},{7,6},{8,7},{9,8},{10,9},{11,1... | collective-permute-start | bytes 98312 | tf_op jit(solution)/shard_map/while/body/eval_jaxpr/ppermute | solution.py:20
  364.8 4.3 collective-permute-start.2
  366.8 6.4 %collective-permute-start.3 = (f32[1,64,128]{2,1,0:T(8,128)S(1)}, f32[1,64,128]{2,1,0:T(8,128)S(1)}, u32[]{:S(2)}, u32[]{:S(2)}) collective-permute-start(f32[1,64,128]{2,1,0:T(8,128)S(1)} %get-tuple-element.300), channel_id=1, source_target_pairs={{1,0},{2,1},{3,2},{4,3},{5,4},{6,5},{7,6},{8,7},{9,8},{10,9},{11,1... | collective-permute-start | bytes 98312 | tf_op jit(solution)/shard_map/while/body/eval_jaxpr/ppermute | solution.py:20
  373.5 4.3 collective-permute-start.2
  375.4 6.4 %collective-permute-start.3 = (f32[1,64,128]{2,1,0:T(8,128)S(1)}, f32[1,64,128]{2,1,0:T(8,128)S(1)}, u32[]{:S(2)}, u32[]{:S(2)}) collective-permute-start(f32[1,64,128]{2,1,0:T(8,128)S(1)} %get-tuple-element.300), channel_id=1, source_target_pairs={{1,0},{2,1},{3,2},{4,3},{5,4},{6,5},{7,6},{8,7},{9,8},{10,9},{11,1... | collective-permute-start | bytes 98312 | tf_op jit(solution)/shard_map/while/body/eval_jaxpr/ppermute | solution.py:20
  384.1 6.4 %collective-permute-start.3 = (f32[1,64,128]{2,1,0:T(8,128)S(1)}, f32[1,64,128]{2,1,0:T(8,128)S(1)}, u32[]{:S(2)}, u32[]{:S(2)}) collective-permute-start(f32[1,64,128]{2,1,0:T(8,128)S(1)} %get-tuple-element.300), channel_id=1, source_target_pairs={{1,0},{2,1},{3,2},{4,3},{5,4},{6,5},{7,6},{8,7},{9,8},{10,9},{11,1... | collective-permute-start | bytes 98312 | tf_op jit(solution)/shard_map/while/body/eval_jaxpr/ppermute | solution.py:20
  392.8 6.4 %collective-permute-start.3 = (f32[1,64,128]{2,1,0:T(8,128)S(1)}, f32[1,64,128]{2,1,0:T(8,128)S(1)}, u32[]{:S(2)}, u32[]{:S(2)}) collective-permute-start(f32[1,64,128]{2,1,0:T(8,128)S(1)} %get-tuple-element.300), channel_id=1, source_target_pairs={{1,0},{2,1},{3,2},{4,3},{5,4},{6,5},{7,6},{8,7},{9,8},{10,9},{11,1... | collective-permute-start | bytes 98312 | tf_op jit(solution)/shard_map/while/body/eval_jaxpr/ppermute | solution.py:20
  401.5 6.4 %collective-permute-start.3 = (f32[1,64,128]{2,1,0:T(8,128)S(1)}, f32[1,64,128]{2,1,0:T(8,128)S(1)}, u32[]{:S(2)}, u32[]{:S(2)}) collective-permute-start(f32[1,64,128]{2,1,0:T(8,128)S(1)} %get-tuple-element.300), channel_id=1, source_target_pairs={{1,0},{2,1},{3,2},{4,3},{5,4},{6,5},{7,6},{8,7},{9,8},{10,9},{11,1... | collective-permute-start | bytes 98312 | tf_op jit(solution)/shard_map/while/body/eval_jaxpr/ppermute | solution.py:20
  408.3 4.3 collective-permute-start.2
  410.2 6.4 %collective-permute-start.3 = (f32[1,64,128]{2,1,0:T(8,128)S(1)}, f32[1,64,128]{2,1,0:T(8,128)S(1)}, u32[]{:S(2)}, u32[]{:S(2)}) collective-permute-start(f32[1,64,128]{2,1,0:T(8,128)S(1)} %get-tuple-element.300), channel_id=1, source_target_pairs={{1,0},{2,1},{3,2},{4,3},{5,4},{6,5},{7,6},{8,7},{9,8},{10,9},{11,1... | collective-permute-start | bytes 98312 | tf_op jit(solution)/shard_map/while/body/eval_jaxpr/ppermute | solution.py:20
  416.9 4.3 collective-permute-start.2
  418.9 6.4 %collective-permute-start.3 = (f32[1,64,128]{2,1,0:T(8,128)S(1)}, f32[1,64,128]{2,1,0:T(8,128)S(1)}, u32[]{:S(2)}, u32[]{:S(2)}) collective-permute-start(f32[1,64,128]{2,1,0:T(8,128)S(1)} %get-tuple-element.300), channel_id=1, source_target_pairs={{1,0},{2,1},{3,2},{4,3},{5,4},{6,5},{7,6},{8,7},{9,8},{10,9},{11,1... | collective-permute-start | bytes 98312 | tf_op jit(solution)/shard_map/while/body/eval_jaxpr/ppermute | solution.py:20
  425.6 4.3 collective-permute-start.2
  427.6 6.4 %collective-permute-start.3 = (f32[1,64,128]{2,1,0:T(8,128)S(1)}, f32[1,64,128]{2,1,0:T(8,128)S(1)}, u32[]{:S(2)}, u32[]{:S(2)}) collective-permute-start(f32[1,64,128]{2,1,0:T(8,128)S(1)} %get-tuple-element.300), channel_id=1, source_target_pairs={{1,0},{2,1},{3,2},{4,3},{5,4},{6,5},{7,6},{8,7},{9,8},{10,9},{11,1... | collective-permute-start | bytes 98312 | tf_op jit(solution)/shard_map/while/body/eval_jaxpr/ppermute | solution.py:20
  (10 other events, 583.2 us)
Sparse Core Ops, SparseCore 0:
  20.7 85.6 all-gather.5
  166.6 89.0 all-gather.3
where the time goes:
time: 445 us; the launch traced here: 442 us
  waiting for transfers between devices  218 us (49%)
  starting transfers between devices  157 us (35%)
  other arithmetic  45.5 us (10%)
  between operations  14.2 us (3%)
    ppermute x33, waiting for transfers between devices, padded_2(): after = lax.ppermute(initial, axis, down)  126 us
    all_gather x2, waiting for transfers between devices, entering(): everything = jax.tree.map(lambda part: lax.all_gather(part, axis), value)  89.2 us
    ppermute x33, starting transfers between devices, padded_2(): after = lax.ppermute(initial, axis, down)  81.1 us
    ppermute x33, starting transfers between devices, padded_2(): before = lax.ppermute(last, axis, up)  72.4 us
    select_n x32, other arithmetic, hop(): return jax.tree.map(lambda a, b: jnp.where(reached, a, b), new, before)  34.3 us
  transfers between devices with their start and end apart: 69, of which 34 were waited for; matrix products, arithmetic and copies ran while one was open for 2% of the time, Pallas kernels for 0%

commit v1 on v0

v1 whole, which is shorter than its diff:
```python
import functools

import jax
import jax.numpy as jnp
from jax import lax
from jax.experimental import pallas as pl
from jax.experimental.pallas import tpu as pltpu
from jax.sharding import PartitionSpec as P

STEPS = 16
REACH = 1
MESH = pl.DeviceIdType.MESH


def kernel(
    n_tm, n_sp, planes, ny, initial_hbm, starts_hbm, k_hbm, corrected_hbm, relaxed_hbm,
    raw, states, work, k1, k2, ends_all, starts_all, corrected_all, out_buf,
    load_sem, store_sem, halo_send, halo_recv, k_send, k_recv, a2a_send, a2a_recv,
):
    nx = raw.shape[-1]
    slab = planes * ny
    halo = REACH * planes
    depth = halo
    rounds = STEPS // depth
    total = planes + 2 * halo
    groups = ny // 8
    chunk = slab // n_tm
    centre = halo * ny
    i = lax.axis_index("tm")
    s = lax.axis_index("space")

    barrier = pltpu.get_barrier_semaphore()
    partners = []
    for d in range(1, REACH + 1):
        partners += [lax.rem(s + d, n_sp), lax.rem(s + n_sp - d, n_sp)]
    for other in partners:
        pl.semaphore_signal(barrier, inc=1, device_id={"space": other}, device_id_type=MESH)

    @pl.loop(1, n_tm)
    def _(d):
        pl.semaphore_signal(
            barrier, inc=1, device_id={"tm": lax.rem(i + d, n_tm)}, device_id_type=MESH
        )

    loads = [
        pltpu.make_async_copy(source, raw.at[n], load_sem.at[n])
        for n, source in enumerate((starts_hbm.at[0], k_hbm, initial_hbm))
    ]
    for load in loads:
        load.start()
    for load in loads:
        load.wait()

    def gathered(n, p, v):
        return raw[n, p, pl.ds(v, 8, stride=groups), :]

    for p in range(planes):
        for v in range(groups):
            row = p * ny + v * 8
            states[0, centre + row : centre + row + 8, :] = gathered(0, p, v)
            k1[centre + row : centre + row + 8, :] = 0.125 * gathered(1, p, v)
            out_buf[0, row : row + 8, :] = gathered(2, p, v)

    pl.semaphore_wait(barrier, 2 * REACH + n_tm - 1)

    def halo_copies(ref, send, recv):
        copies = []
        for d in range(1, REACH + 1):
            for side, other, start in (
                (0, lax.rem(s + d, n_sp), centre - d * slab),
                (1, lax.rem(s + n_sp - d, n_sp), centre + d * slab),
            ):
                n = 2 * (d - 1) + side
                copies.append(
                    pltpu.make_async_remote_copy(
                        src_ref=ref.at[pl.ds(centre, slab)],
                        dst_ref=ref.at[pl.ds(start, slab)],
                        send_sem=send.at[n],
                        recv_sem=recv.at[n],
                        device_id={"space": other},
                        device_id_type=MESH,
                    )
                )
        return copies

    def state_copies(slot):
        return halo_copies(states.at[slot], halo_send.at[slot], halo_recv.at[slot])

    def scatter_copy(kind, source, target, d):
        return pltpu.make_async_remote_copy(
            src_ref=source,
            dst_ref=target,
            send_sem=a2a_send.at[kind, d],
            recv_sem=a2a_recv.at[kind, d],
            device_id={"tm": lax.rem(i + d, n_tm)},
            device_id_type=MESH,
        )

    def rows_of(index, base=0):
        return pl.ds(pl.multiple_of(base + index * chunk, 8), chunk)

    def starts_copy(d):
        j = lax.rem(i + d, n_tm)
        return scatter_copy(0, states.at[0, rows_of(j, centre)], starts_all.at[rows_of(i)], d)

    def ends_copy(d):
        j = lax.rem(i + d, n_tm)
        return scatter_copy(1, states.at[rounds, rows_of(j, centre)], ends_all.at[rows_of(i)], d)

    def corrected_copy(d):
        j = lax.rem(i + d, n_tm)
        return scatter_copy(
            2, corrected_all.at[rows_of(j)], states.at[rounds + 1, rows_of(i, centre)], d
        )

    def all_partners(action):
        @pl.loop(1, n_tm)
        def _(d):
            action(d)

    k_copies = halo_copies(k1, k_send, k_recv)
    for a, b in zip(k_copies, state_copies(0)):
        a.start()
        b.start()
    all_partners(lambda d: starts_copy(d).start())
    starts_all[rows_of(i), :] = states[0, rows_of(i, centre), :]

    left = [None] + [jnp.where(s >= d, 1.0, 0.0).astype(jnp.float32) for d in range(1, REACH + 1)]
    right = [None] + [
        jnp.where(s + d < n_sp, 1.0, 0.0).astype(jnp.float32) for d in range(1, REACH + 1)
    ]

    def inside(p):
        if p < halo:
            return left[(halo - p + planes - 1) // planes]
        if p >= halo + planes:
            return right[(p - halo) // planes]
        return None

    def edge(p):
        return (p < halo and (halo - 1 - p) % planes == 0) or (
            p >= halo + planes and (p - halo) % planes == 0
        )

    def at(p):
        return slice(p * ny, (p + 1) * ny)

    for a in k_copies:
        a.wait()
    for p in range(total):
        k = k1[at(p), :]
        mask = inside(p)
        if mask is not None:
            k = k * mask
            k1[at(p), :] = k
        k2[at(p), :] = 0.25 * k

    lane = lax.broadcasted_iota(jnp.int32, (ny, nx), 1)
    first_lane = lane == 0
    last_lane = lane == nx - 1
    sublane = lax.broadcasted_iota(jnp.int32, (8, nx), 0)
    first_row = sublane == 0
    last_row = sublane == 7

    def above(x):
        end = jnp.where(last_row, 0.0, pltpu.roll(x[:8], 7, 0))
        return jnp.concatenate([x[8:], end], axis=0)

    def advance(read, write, lo, hi):
        def plane(p):
            u = read(p)
            return u, k1[at(p), :] + k2[at(p), :] * jnp.tanh(u)

        u, a = plane(lo - 1)
        next_u, next_a = plane(lo)
        below = (a + next_a) * (next_u - u)
        for p in range(lo, hi):
            u, a = next_u, next_a
            next_u, next_a = plane(p + 1)
            flux_z = (a + next_a) * (next_u - u)
            flux_y = (a + above(a)) * (above(u) - u)
            own = a * u
            low_y = jnp.concatenate(
                [jnp.where(first_row, own[:8], pltpu.roll(flux_y[-8:], 1, 0)), flux_y[:-8]], axis=0
            )
            beside_u = jnp.where(last_lane, 0.0, pltpu.roll(u, nx - 1, 1))
            beside_a = jnp.where(last_lane, 0.0, pltpu.roll(a, nx - 1, 1))
            flux_x = (a + beside_a) * (beside_u - u)
            low_x = jnp.where(first_lane, own, pltpu.roll(flux_x, 1, 1))
            new = u + (((flux_x - low_x) + (flux_y - low_y)) + 4.0 * (flux_z - below))
            if edge(p):
                new = new * inside(p)
            write(p, new)
            below = flux_z

    def relax_round(slot):
        for t in range(1, depth + 1):

            def read(p, t=t):
                if t > 1:
                    return work[at(p), :]
                u = states[slot, at(p), :]
                mask = inside(p)
                return u if mask is None else u * mask

            def write(p, value, t=t):
                if t < depth:
                    work[at(p), :] = value
                else:
                    states[slot + 1, at(p), :] = value

            advance(read, write, t, total - t)

    def relax(base):
        @pl.loop(0, rounds)
        def _(r):
            slot = base + r
            for copy in state_copies(slot):
                copy.wait()
            relax_round(slot)

            @pl.when(r < rounds - 1)
            def _():
                for copy in state_copies(slot + 1):
                    copy.start()

    relax(0)

    all_partners(lambda d: ends_copy(d).start())
    ends_all[rows_of(i), :] = states[rounds, rows_of(i, centre), :]
    all_partners(lambda d: starts_copy(d).wait())
    all_partners(lambda d: ends_copy(d).wait())

    damping = 1.0 / (1.0 + (STEPS * 3.0 * 8.0) * k1[rows_of(i, centre), :])
    begin = starts_all[0:chunk, :]
    error = out_buf[0, rows_of(i), :] - begin
    corrected_all[0:chunk, :] = begin + error
    for j in range(1, n_tm):
        begin = starts_all[j * chunk : (j + 1) * chunk, :]
        jump = ends_all[(j - 1) * chunk : j * chunk, :] - begin
        error = damping * error + jump
        corrected_all[j * chunk : (j + 1) * chunk, :] = begin + error

    all_partners(lambda d: corrected_copy(d).start())
    states[rounds + 1, rows_of(i, centre), :] = corrected_all[rows_of(i), :]
    all_partners(lambda d: corrected_copy(d).wait())

    for copy in state_copies(rounds + 1):
        copy.start()

    def restore(slot, n, target):
        for p in range(planes):
            for v in range(groups):
                row = centre + p * ny + v * 8
                raw[n, p, pl.ds(v, 8, stride=groups), :] = states[slot, row : row + 8, :]
        copy = pltpu.make_async_copy(raw.at[n], target.at[0], store_sem.at[n])
        copy.start()
        return copy

    first = restore(rounds + 1, 0, corrected_hbm)
    relax(rounds + 1)
    second = restore(2 * rounds + 1, 1, relaxed_hbm)
    first.wait()
    second.wait()


def solution(mesh):
    n_tm, n_sp = mesh.shape["tm"], mesh.shape["space"]

    def on_device(initial, starts, conductivity):
        planes, ny, nx = initial.shape
        slab = planes * ny
        halo = REACH * planes
        total = planes + 2 * halo
        slots = 2 * (STEPS // halo + 1)
        f32 = jnp.float32
        out = jax.ShapeDtypeStruct(starts.shape, f32)
        return pl.pallas_call(
            functools.partial(kernel, n_tm, n_sp, planes, ny),
            out_shape=(out, out),
            in_specs=[pl.BlockSpec(memory_space=pl.ANY)] * 3,
            out_specs=[pl.BlockSpec(memory_space=pl.ANY)] * 2,
            scratch_shapes=[
                pltpu.VMEM((3, planes, ny, nx), f32),
                pltpu.VMEM((slots, total * ny, nx), f32),
                pltpu.VMEM((total * ny, nx), f32),
                pltpu.VMEM((total * ny, nx), f32),
                pltpu.VMEM((total * ny, nx), f32),
                pltpu.VMEM((slab, nx), f32),
                pltpu.VMEM((slab, nx), f32),
                pltpu.VMEM((slab, nx), f32),
                pltpu.VMEM((1, slab, nx), f32),
                pltpu.SemaphoreType.DMA((3,)),
                pltpu.SemaphoreType.DMA((2,)),
                pltpu.SemaphoreType.DMA((slots, 2 * REACH)),
                pltpu.SemaphoreType.DMA((slots, 2 * REACH)),
                pltpu.SemaphoreType.DMA((2 * REACH,)),
                pltpu.SemaphoreType.DMA((2 * REACH,)),
                pltpu.SemaphoreType.DMA((3, n_tm)),
                pltpu.SemaphoreType.DMA((3, n_tm)),
            ],
            compiler_params=pltpu.CompilerParams(collective_id=0, has_side_effects=True),
        )(initial, starts, conductivity)

    in_specs = (P("space", None, None), P("tm", "space", None, None), P("space", None, None))
    out_specs = (P("tm", "space", None, None), P("tm", "space", None, None))
    return jax.shard_map(
        on_device, mesh=mesh, in_specs=in_specs, out_specs=out_specs, check_vma=False
    )
```

time: 445 us -> 85.5 us (0.19)
  waiting for transfers between devices: 218 us -> 0 us
  starting transfers between devices: 157 us -> 0 us
  Pallas kernels: 0 us -> 80.9 us
  other arithmetic: 45.5 us -> 0 us
  between operations: 14.2 us -> 0.65 us
    ppermute x67 -> x0, starting transfers between devices: 157 us -> none  [the longest x33 81.1 us: padded_2(): after = lax.ppermute(initial, axis, down)]
    ppermute x67 -> x0, waiting for transfers between devices: 128 us -> none  [the longest x33 126 us: padded_2(): after = lax.ppermute(initial, axis, down)]
    all_gather x2 -> x0, waiting for transfers between devices: 89.2 us -> none  [entering(): everything = jax.tree.map(lambda part: lax.all_gather(part, axis), value)]
    pallas_call x0 -> x1, Pallas kernels: none -> 80.9 us  [on_device(): pl.pallas_call(functools.partial(kernel, n_tm, n_sp, planes, ny), out_sha...]
    select_n x32 -> x0, other arithmetic: 34.3 us -> none  [hop(): return jax.tree.map(lambda a, b: jnp.where(reached, a, b), new, before)]
    add x33 -> x0, other arithmetic: 7.81 us -> none  [the longest x32 6.87 us: advance(): return centre + change]
  transfers between devices with their start and end apart: 69 -> 0, of which waited for: 34 -> 0; matrix products, arithmetic and copies ran while one was open for 2% -> 0% of each run, Pallas kernels for 0% -> 0%
where the time goes in v1:
time: 85.5 us; the launch traced here: 83.8 us
  Pallas kernels  80.9 us (95%)
  local copies, waits for them, and re-layouts  2.26 us (3%)
    pallas_call x1, Pallas kernels, on_device(): pl.pallas_call(functools.partial(kernel, n_tm, n_sp, planes, ny), out_sha...  80.9 us
    unnamed x4, local copies, waits for them, and re-layouts  2.26 us

profile of v1, /device:TPU:1, one launch (start us, length us, event | category | flops | bytes accessed | tf_op | source)
XLA Modules:
  0.0 83.8 jit_solution(1653703258060028530)
XLA Ops:
  0.6 80.9 %shard_map.50 = (f32[1,4,64,128]{3,2,1,0:T(8,128)}, f32[1,4,64,128]{3,2,1,0:T(8,128)}) custom-call(f32[4,64,128]{2,1,0:T(8,128)} %initial_hbm.1, f32[1,4,64,128]{3,2,1,0:T(8,128)} %starts_hbm.1, f32[4,64,128]{2,1,0:T(8,128)} %k_hbm.1), custom_call_target="tpu_custom_call" | custom-call | tf_op jit(solution)/shard_map/pallas_call | solution.py:278
  81.5 0.0 copy-start
  81.5 1.6 %copy.7 = f32[1,4,64,128]{3,2,1,0:T(8,128)} copy(f32[1,4,64,128]{3,2,1,0:T(8,128)} %get-tuple-element.4) | data formatting | bytes 262144
  83.2 0.0 copy-done
  83.2 0.7 copy.8
Async XLA Ops:
  81.5 1.6 %copy-start = (f32[1,4,64,128]{3,2,1,0:T(8,128)S(1)}, f32[1,4,64,128]{3,2,1,0:T(8,128)}, u32[]{:S(2)}) copy-start(f32[1,4,64,128]{3,2,1,0:T(8,128)} %get-tuple-element.5) | copy-start | bytes 393220

commit v2 on v0

v2 whole, which is shorter than its diff:
```python
import functools

import jax
import jax.numpy as jnp
from jax import lax
from jax.experimental import pallas as pl
from jax.experimental.pallas import tpu as pltpu
from jax.sharding import PartitionSpec as P

STEPS = 16
FAR = 8
NEAR = 4
OWN = 4
ROUNDS = STEPS // FAR
TOTAL = FAR + OWN + NEAR
END = ROUNDS
AGAIN = ROUNDS + 1
LAST = AGAIN + ROUNDS
MESH = pl.DeviceIdType.MESH


def kernel(
    n_tm, n_sp, ny, initial_hbm, starts_hbm, k_hbm, corrected_hbm, relaxed_hbm,
    raw, state, middle, level_u, level_a, k_in, k1, k2,
    ends_all, starts_all, corrected_all, first_all,
    load_sem, store_sem, halo_send, halo_recv, mid_send, mid_recv, a2a_send, a2a_recv,
):
    nx = raw.shape[-1]
    slab = OWN * ny
    groups = ny // 8
    chunk = slab // n_tm
    base = FAR * ny
    i = lax.axis_index("tm")
    s = lax.axis_index("space")
    odd = lax.rem(s, 2)
    turn = 1 - 2 * odd
    facing = lax.rem(s + n_sp - turn, n_sp)
    behind = lax.rem(s + n_sp + 2 * turn, n_sp)
    ahead = lax.rem(s + n_sp - 2 * turn, n_sp)
    sibling = s + turn

    barrier = pltpu.get_barrier_semaphore()
    for other in (facing, behind, ahead, sibling):
        pl.semaphore_signal(barrier, inc=1, device_id={"space": other}, device_id_type=MESH)

    @pl.loop(1, n_tm)
    def _(d):
        pl.semaphore_signal(
            barrier, inc=1, device_id={"tm": lax.rem(i + d, n_tm)}, device_id_type=MESH
        )

    loads = [
        pltpu.make_async_copy(source, raw.at[n], load_sem.at[n])
        for n, source in enumerate((starts_hbm.at[0], k_hbm, initial_hbm))
    ]
    for load in loads:
        load.start()
    for load in loads:
        load.wait()

    lane = lax.broadcasted_iota(jnp.int32, (8, nx), 1)
    sublane = lax.broadcasted_iota(jnp.int32, (8, nx), 0)
    split = (lane % 16) * 8 + (8 - lane // 16) % 8
    flip = (8 - lane // 16) % 8 * 16 + lane % 16
    join = (lane % 8) * 16 + lane // 8

    def permuted(x, index):
        return jnp.take_along_axis(x, index, axis=1)

    def exchanged(x):
        x = pltpu.roll(x, 0, 1, stride=16, stride_axis=0)
        for bit in (1, 2, 4):
            x = jnp.where((lane // 16) & bit != 0, pltpu.roll(x, 8 - bit, 0), x)
        return pltpu.roll(x, 0, 1, stride=16, stride_axis=0)

    def taken_in(x):
        return exchanged(permuted(x, split))

    def given_out(x):
        return permuted(exchanged(permuted(x, flip)), join)

    def raw_rows(n, p, v):
        return n, p * turn + (OWN - 1) * odd, pl.ds(v, 8, stride=groups), slice(None)

    for p in range(OWN):
        for v in range(groups):
            row = p * ny + v * 8
            state[0, base + row : base + row + 8, :] = taken_in(raw[raw_rows(0, p, v)])
            k_in[base + row : base + row + 8, :] = 0.125 * taken_in(raw[raw_rows(1, p, v)])

    pl.semaphore_wait(barrier, 4 + n_tm - 1)

    def planes(p, n=1):
        return pl.ds(p * ny, n * ny)

    def hop(ref, start, stop, n, other, send, recv):
        return pltpu.make_async_remote_copy(
            src_ref=ref.at[planes(start, n)],
            dst_ref=ref.at[planes(stop, n)],
            send_sem=send,
            recv_sem=recv,
            device_id={"space": other},
            device_id_type=MESH,
        )

    def across(ref, q):
        return [
            hop(ref, FAR + p, FAR - 1 - p, 1, facing, halo_send.at[q, p], halo_recv.at[q, p])
            for p in range(OWN)
        ]

    def beyond(ref, q):
        return [
            hop(ref, FAR + p, p, 2, behind, halo_send.at[q, n], halo_recv.at[q, n])
            for n, p in ((4, 2), (5, 0))
        ]

    def beside(ref, send, recv):
        return [
            hop(ref, FAR + p, TOTAL - 1 - p, 1, sibling, send(p), recv(p)) for p in range(OWN)
        ]

    def beside_start(ref, q):
        return beside(ref, lambda p: halo_send.at[q, 6 + p], lambda p: halo_recv.at[q, 6 + p])

    def beside_middle(q):
        return beside(middle.at[q], lambda p: mid_send.at[q, p], lambda p: mid_recv.at[q, p])

    for n in range(chunk // 8):
        part = i * (chunk // 8) + n
        first_all[n * 8 : n * 8 + 8, :] = taken_in(raw[raw_rows(2, part // groups, part % groups)])

    def rows_of(index, start=0):
        return pl.ds(pl.multiple_of(start + index * chunk, 8), chunk)

    def scatter_copy(kind, source, target, d):
        return pltpu.make_async_remote_copy(
            src_ref=source,
            dst_ref=target,
            send_sem=a2a_send.at[kind, d],
            recv_sem=a2a_recv.at[kind, d],
            device_id={"tm": lax.rem(i + d, n_tm)},
            device_id_type=MESH,
        )

    def starts_copy(d):
        j = lax.rem(i + d, n_tm)
        return scatter_copy(0, state.at[0, rows_of(j, base)], starts_all.at[rows_of(i)], d)

    def ends_copy(d):
        j = lax.rem(i + d, n_tm)
        return scatter_copy(1, state.at[END, rows_of(j, base)], ends_all.at[rows_of(i)], d)

    def corrected_copy(d):
        j = lax.rem(i + d, n_tm)
        return scatter_copy(2, corrected_all.at[rows_of(j)], state.at[AGAIN, rows_of(i, base)], d)

    def all_partners(action):
        @pl.loop(1, n_tm)
        def _(d):
            action(d)

    K = LAST + 1
    k_copies = across(k_in, K) + beyond(k_in, K) + beside_start(k_in, K)

    def send_start(slot):
        for copy in beside_start(state.at[slot], slot) + across(state.at[slot], slot):
            copy.start()

    for copy in k_copies:
        copy.start()
    send_start(0)
    all_partners(lambda d: starts_copy(d).start())
    starts_all[rows_of(i), :] = state[0, rows_of(i, base), :]

    end = jnp.where(odd == 0, s == 0, s == n_sp - 1)
    inside = jnp.where(end, 0.0, 1.0).astype(jnp.float32)

    def at(p, v):
        return slice((p + FAR) * ny + v * 8, (p + FAR) * ny + v * 8 + 8)

    for copy in k_copies:
        copy.wait()
    for p in range(-FAR, OWN + NEAR):
        for v in range(groups):
            k = k_in[at(p, v), :]
            if p < 0:
                k = k * inside
            k1[at(p, v), :] = k
            k2[at(p, v), :] = 0.25 * k

    first_x = lane % 16 == 0
    last_x = lane % 16 == 15
    first_y = lane < 16
    last_y = lane >= nx - 16

    def diffusivity(p, v, u):
        return k1[at(p, v), :] + k2[at(p, v), :] * jnp.tanh(u)

    def relax(first_slot):
        @pl.loop(0, ROUNDS)
        def _(r):
            slot = first_slot + r
            q = r + (ROUNDS if first_slot else 0)

            def wide(p, v, shift=0):
                row = ((p + FAR) * groups + v) * 16 + 8 + shift
                return slice(row, row + 8)

            def wide_all(p, shift):
                return pl.ds((p + FAR) * groups * 16 + 8 + shift, 8, stride=16)

            def put(t, p, v, u):
                if t == FAR:
                    state[slot + 1, at(p, v), :] = u
                    return
                level_u[t, wide(p, v), :] = u
                level_a[t, wide(p, v), :] = diffusivity(p, v, u)
                if t == 4 and 0 <= p < OWN:
                    middle[q, at(p, v), :] = u

            def close(t, p):
                if t == FAR:
                    return
                for ref in (level_u, level_a):
                    after = pltpu.roll(ref[t, wide_all(p, 0), :], nx - 1, 1)
                    before = pltpu.roll(ref[t, wide_all(p, 7), :], 1, 1)
                    ref[t, wide_all(p, 8), :] = jnp.where(last_x, 0.0, after)
                    ref[t, wide_all(p, -1), :] = jnp.where(first_x, 0.0, before)

            def ingest(p):
                for v in range(groups):
                    u = state[slot, at(p, v), :]
                    put(0, p, v, u * inside if p < 0 else u)
                close(0, p)

            def strip(t, lo, hi):
                def old(p, v, shift=0):
                    rows = wide(p, v, shift)
                    return level_u[t - 1, rows, :], level_a[t - 1, rows, :]

                def flux(here, there):
                    return (here[1] + there[1]) * (there[0] - here[0])

                below = [None] * groups
                for p in range(lo, hi + 1):
                    cells = [old(p, v) for v in range(groups)]
                    over = tuple(
                        jnp.where(last_y, 0.0, pltpu.roll(x, nx - 16, 1)) for x in cells[0]
                    )
                    top = flux(cells[-1], over)
                    low_y = jnp.where(
                        first_y, cells[0][0] * cells[0][1], pltpu.roll(top, 16, 1)
                    )
                    for v in range(groups):
                        here = cells[v]
                        if p == lo:
                            below[v] = flux(old(p - 1, v), here)
                        flux_z = flux(here, old(p + 1, v))
                        flux_y = top if v == groups - 1 else flux(here, cells[v + 1])
                        flux_x = flux(here, old(p, v, 1)) + flux(here, old(p, v, -1))
                        new = here[0] + (
                            (flux_x + (flux_y - low_y)) + 4.0 * (flux_z - below[v])
                        )
                        if p == -1:
                            new = new * inside
                        put(t, p, v, new)
                        below[v], low_y = flux_z, flux_y
                    close(t, p)

            side, cross, far = (
                beside_start(state.at[slot], slot),
                across(state.at[slot], slot),
                beyond(state.at[slot], slot),
            )
            mid = beside_middle(q)
            for p in range(OWN):
                ingest(p)
            for copy in side:
                copy.wait_recv()
            for copy in far:
                copy.start()
            for p in range(OWN, OWN + NEAR):
                ingest(p)
            strip(1, 1, 6)
            strip(2, 2, 5)
            strip(3, 3, 4)
            for n, arrivals in enumerate((cross[:2], cross[2:], far[:1], far[1:])):
                for copy in arrivals:
                    copy.wait_recv()
                ingest(-1 - 2 * n)
                ingest(-2 - 2 * n)
                for t in range(1, 5):
                    strip(t, t - 2 - 2 * n, t - 1 - 2 * n)
                if n == 0:
                    mid[3].start()
                    mid[2].start()
                if n == 1:
                    mid[1].start()
                    mid[0].start()
            strip(5, -3, 2)
            strip(6, -2, 1)
            strip(7, -1, 0)
            for copy in mid:
                copy.wait_recv()
            for p in range(OWN, OWN + NEAR):
                for v in range(groups):
                    put(4, p, v, middle[q, at(p, v), :])
                close(4, p)
            strip(5, 3, 6)
            strip(6, 2, 5)
            strip(7, 1, 4)
            strip(8, 0, 3)

            @pl.when(r < ROUNDS - 1)
            def _():
                send_start(slot + 1)

            for copy in side + cross + far + mid:
                copy.wait_send()

    relax(0)

    all_partners(lambda d: ends_copy(d).start())
    ends_all[rows_of(i), :] = state[END, rows_of(i, base), :]
    all_partners(lambda d: starts_copy(d).wait())
    all_partners(lambda d: ends_copy(d).wait())

    damping = 1.0 / (1.0 + (STEPS * 3.0 * 8.0) * k_in[rows_of(i, base), :])
    begin = starts_all[0:chunk, :]
    error = first_all[...] - begin
    corrected_all[0:chunk, :] = begin + error
    for j in range(1, n_tm):
        begin = starts_all[j * chunk : (j + 1) * chunk, :]
        jump = ends_all[(j - 1) * chunk : j * chunk, :] - begin
        error = damping * error + jump
        corrected_all[j * chunk : (j + 1) * chunk, :] = begin + error

    all_partners(lambda d: corrected_copy(d).start())
    state[AGAIN, rows_of(i, base), :] = corrected_all[rows_of(i), :]
    all_partners(lambda d: corrected_copy(d).wait())

    send_start(AGAIN)

    def restore(slot, n, target):
        for p in range(OWN):
            for v in range(groups):
                raw[raw_rows(n, p, v)] = given_out(state[slot, at(p, v), :])
        copy = pltpu.make_async_copy(raw.at[n], target.at[0], store_sem.at[n])
        copy.start()
        return copy

    first = restore(AGAIN, 0, corrected_hbm)
    relax(AGAIN)
    second = restore(LAST, 1, relaxed_hbm)
    first.wait()
    second.wait()


def solution(mesh):
    n_tm, n_sp = mesh.shape["tm"], mesh.shape["space"]

    def on_device(initial, starts, conductivity):
        own, ny, nx = initial.shape
        slab = own * ny
        f32 = jnp.float32
        out = jax.ShapeDtypeStruct(starts.shape, f32)
        region = (TOTAL * ny, nx)
        return pl.pallas_call(
            functools.partial(kernel, n_tm, n_sp, ny),
            out_shape=(out, out),
            in_specs=[pl.BlockSpec(memory_space=pl.ANY)] * 3,
            out_specs=[pl.BlockSpec(memory_space=pl.ANY)] * 2,
            scratch_shapes=[
                pltpu.VMEM((3, own, ny, nx), f32),
                pltpu.VMEM((LAST + 1, *region), f32),
                pltpu.VMEM((2 * ROUNDS, *region), f32),
                pltpu.VMEM((FAR, 2 * TOTAL * ny + 8, nx), f32),
                pltpu.VMEM((FAR, 2 * TOTAL * ny + 8, nx), f32),
                pltpu.VMEM(region, f32),
                pltpu.VMEM(region, f32),
                pltpu.VMEM(region, f32),
                pltpu.VMEM((slab, nx), f32),
                pltpu.VMEM((slab, nx), f32),
                pltpu.VMEM((slab, nx), f32),
                pltpu.VMEM((slab // n_tm, nx), f32),
                pltpu.SemaphoreType.DMA((3,)),
                pltpu.SemaphoreType.DMA((2,)),
                pltpu.SemaphoreType.DMA((LAST + 2, 10)),
                pltpu.SemaphoreType.DMA((LAST + 2, 10)),
                pltpu.SemaphoreType.DMA((2 * ROUNDS, OWN)),
                pltpu.SemaphoreType.DMA((2 * ROUNDS, OWN)),
                pltpu.SemaphoreType.DMA((3, n_tm)),
                pltpu.SemaphoreType.DMA((3, n_tm)),
            ],
            compiler_params=pltpu.CompilerParams(collective_id=0, has_side_effects=True),
        )(initial, starts, conductivity)

    in_specs = (P("space", None, None), P("tm", "space", None, None), P("space", None, None))
    out_specs = (P("tm", "space", None, None), P("tm", "space", None, None))
    return jax.shard_map(
        on_device, mesh=mesh, in_specs=in_specs, out_specs=out_specs, check_vma=False
    )
```

time: 445 us -> 72.7 us (0.16)
  waiting for transfers between devices: 218 us -> 0 us
  starting transfers between devices: 157 us -> 0 us
  Pallas kernels: 0 us -> 69.6 us
  other arithmetic: 45.5 us -> 0 us
  between operations: 14.2 us -> 0.65 us
    ppermute x67 -> x0, starting transfers between devices: 157 us -> none  [the longest x33 81.1 us: padded_2(): after = lax.ppermute(initial, axis, down)]
    ppermute x67 -> x0, waiting for transfers between devices: 128 us -> none  [the longest x33 126 us: padded_2(): after = lax.ppermute(initial, axis, down)]
    all_gather x2 -> x0, waiting for transfers between devices: 89.2 us -> none  [entering(): everything = jax.tree.map(lambda part: lax.all_gather(part, axis), value)]
    pallas_call x0 -> x1, Pallas kernels: none -> 69.6 us  [on_device(): pl.pallas_call(functools.partial(kernel, n_tm, n_sp, ny), out_shape=(out,...]
    select_n x32 -> x0, other arithmetic: 34.3 us -> none  [hop(): return jax.tree.map(lambda a, b: jnp.where(reached, a, b), new, before)]
    add x33 -> x0, other arithmetic: 7.81 us -> none  [the longest x32 6.87 us: advance(): return centre + change]
  transfers between devices with their start and end apart: 69 -> 0, of which waited for: 34 -> 0; matrix products, arithmetic and copies ran while one was open for 2% -> 0% of each run, Pallas kernels for 0% -> 0%
where the time goes in v2:
time: 72.7 us; the launch traced here: 72.6 us
  Pallas kernels  69.6 us (96%)
  local copies, waits for them, and re-layouts  2.26 us (3%)
    pallas_call x1, Pallas kernels, on_device(): pl.pallas_call(functools.partial(kernel, n_tm, n_sp, ny), out_shape=(out,...  69.6 us
    unnamed x4, local copies, waits for them, and re-layouts  2.26 us

profile of v2, /device:TPU:1, one launch (start us, length us, event | category | flops | bytes accessed | tf_op | source)
XLA Modules:
  0.0 72.6 jit_solution(12796011407379093060)
XLA Ops:
  0.6 69.6 %shard_map.50 = (f32[1,4,64,128]{3,2,1,0:T(8,128)}, f32[1,4,64,128]{3,2,1,0:T(8,128)}) custom-call(f32[4,64,128]{2,1,0:T(8,128)} %initial_hbm.1, f32[1,4,64,128]{3,2,1,0:T(8,128)} %starts_hbm.1, f32[4,64,128]{2,1,0:T(8,128)} %k_hbm.1), custom_call_target="tpu_custom_call" | custom-call | tf_op jit(solution)/shard_map/pallas_call | solution.py:369
  70.3 0.0 copy-start
  70.3 1.6 %copy.7 = f32[1,4,64,128]{3,2,1,0:T(8,128)} copy(f32[1,4,64,128]{3,2,1,0:T(8,128)} %get-tuple-element.4) | data formatting | bytes 262144
  71.9 0.0 copy-done
  71.9 0.7 copy.8
Async XLA Ops:
  70.3 1.6 %copy-start = (f32[1,4,64,128]{3,2,1,0:T(8,128)S(1)}, f32[1,4,64,128]{3,2,1,0:T(8,128)}, u32[]{:S(2)}) copy-start(f32[1,4,64,128]{3,2,1,0:T(8,128)} %get-tuple-element.5) | copy-start | bytes 393220

commit v3 on v2

--- a/solution.py
+++ b/solution.py
@@ -31,6 +31,8 @@
     chunk = slab // n_tm
     base = FAR * ny
     i = lax.axis_index("tm")
+    n_x = n_tm // 8 if n_tm >= 16 else 2
+    n_y = n_tm // n_x
     s = lax.axis_index("space")
     odd = lax.rem(s, 2)
     turn = 1 - 2 * odd
@@ -133,30 +135,38 @@
     def rows_of(index, start=0):
         return pl.ds(pl.multiple_of(start + index * chunk, 8), chunk)
 
+    def outward(n, size):
+        return size // 2 + (n + 1) // 2 * (1 - 2 * lax.rem(n, 2))
+
+    def partner(d):
+        y = lax.rem(i // n_x + outward(d // n_x, n_y), n_y)
+        x = lax.rem(lax.rem(i, n_x) + outward(lax.rem(d, n_x), n_x), n_x)
+        return y * n_x + x
+
     def scatter_copy(kind, source, target, d):
         return pltpu.make_async_remote_copy(
             src_ref=source,
             dst_ref=target,
             send_sem=a2a_send.at[kind, d],
             recv_sem=a2a_recv.at[kind, d],
-            device_id={"tm": lax.rem(i + d, n_tm)},
+            device_id={"tm": partner(d)},
             device_id_type=MESH,
         )
 
     def starts_copy(d):
-        j = lax.rem(i + d, n_tm)
+        j = partner(d)
         return scatter_copy(0, state.at[0, rows_of(j, base)], starts_all.at[rows_of(i)], d)
 
     def ends_copy(d):
-        j = lax.rem(i + d, n_tm)
+        j = partner(d)
         return scatter_copy(1, state.at[END, rows_of(j, base)], ends_all.at[rows_of(i)], d)
 
     def corrected_copy(d):
-        j = lax.rem(i + d, n_tm)
+        j = partner(d)
         return scatter_copy(2, corrected_all.at[rows_of(j)], state.at[AGAIN, rows_of(i, base)], d)
 
     def all_partners(action):
-        @pl.loop(1, n_tm)
+        @pl.loop(0, n_tm - 1)
         def _(d):
             action(d)
 
@@ -164,7 +174,7 @@
     k_copies = across(k_in, K) + beyond(k_in, K) + beside_start(k_in, K)
 
     def send_start(slot):
-        for copy in beside_start(state.at[slot], slot) + across(state.at[slot], slot):
+        for copy in across(state.at[slot], slot) + beside_start(state.at[slot], slot) + beyond(state.at[slot], slot):
             copy.start()
 
     for copy in k_copies:
@@ -278,8 +288,6 @@
                 ingest(p)
             for copy in side:
                 copy.wait_recv()
-            for copy in far:
-                copy.start()
             for p in range(OWN, OWN + NEAR):
                 ingest(p)
             strip(1, 1, 6)

time: 72.7 us -> 68.3 us (0.939)
  Pallas kernels: 69.6 us -> 65.3 us
    pallas_call x1, Pallas kernels: 69.6 us -> 65.3 us  [on_device(): pl.pallas_call(functools.partial(kernel, n_tm, n_sp, ny), out_shape=(out,...]
where the time goes in v3:
time: 68.3 us; the launch traced here: 68.2 us
  Pallas kernels  65.3 us (96%)
  local copies, waits for them, and re-layouts  2.26 us (3%)
    pallas_call x1, Pallas kernels, on_device(): pl.pallas_call(functools.partial(kernel, n_tm, n_sp, ny), out_shape=(out,...  65.3 us
    unnamed x4, local copies, waits for them, and re-layouts  2.26 us

profile of v3, /device:TPU:1, one launch (start us, length us, event | category | flops | bytes accessed | tf_op | source)
XLA Modules:
  0.0 68.2 jit_solution(12879485122699812779)
XLA Ops:
  0.6 65.3 %shard_map.50 = (f32[1,4,64,128]{3,2,1,0:T(8,128)}, f32[1,4,64,128]{3,2,1,0:T(8,128)}) custom-call(f32[4,64,128]{2,1,0:T(8,128)} %initial_hbm.1, f32[1,4,64,128]{3,2,1,0:T(8,128)} %starts_hbm.1, f32[4,64,128]{2,1,0:T(8,128)} %k_hbm.1), custom_call_target="tpu_custom_call" | custom-call | tf_op jit(solution)/shard_map/pallas_call | solution.py:377
  65.9 0.0 copy-start
  65.9 1.6 %copy.7 = f32[1,4,64,128]{3,2,1,0:T(8,128)} copy(f32[1,4,64,128]{3,2,1,0:T(8,128)} %get-tuple-element.4) | data formatting | bytes 262144
  67.5 0.0 copy-done
  67.5 0.7 copy.8
Async XLA Ops:
  65.9 1.6 %copy-start = (f32[1,4,64,128]{3,2,1,0:T(8,128)S(1)}, f32[1,4,64,128]{3,2,1,0:T(8,128)}, u32[]{:S(2)}) copy-start(f32[1,4,64,128]{3,2,1,0:T(8,128)} %get-tuple-element.5) | copy-start | bytes 393220
